TPU v7x, 32 devices: a whole 2x2x4 slice. The times are simulated.
32 devices in a mesh: gx: 8 (over y, x, core), gy: 4 (over z).
Axes of the slice: x: 2, y: 2, z: 4, core: 2. Of those that a mesh axis runs over, the one named last changes fastest.
Arguments:
- elevation: float32 [8, 128, 1024], P(None, 'gy', 'gx'), may hold values from -4 to 4
- east_velocity: float32 [8, 128, 1024], P(None, 'gy', 'gx'), may hold values from -3 to 3
- north_velocity: float32 [8, 128, 1024], P(None, 'gy', 'gx'), may hold values from -3 to 3
- water_depth: float32 [128, 1024], P('gy', 'gx'), may hold values from 0.3 to 1
- land_sea: int32 [128, 1024], P('gy', 'gx'), may hold values 0 or 1
Outputs:
- surface: float32 [8, 128, 1024], P(None, 'gy', 'gx')
- east_flow: float32 [8, 128, 1024], P(None, 'gy', 'gx')
- north_flow: float32 [8, 128, 1024], P(None, 'gy', 'gx')
- loading: float32 [8, 16, 128], P(None, 'gy', 'gx')
All inputs are finite; a program needn't handle non-finite values. No bound on the sum of `land_sea` on one device may be relied on, other than what follows from the above.
Results may differ from a plain program's by a relative error of at most 0.0032.
Values may be sent and summed in bfloat16 or wider, within the bound.
A program may use at most 64 MiB of HBM per device.

v0:
```python
import functools
import math

import jax
import jax.numpy as jnp
from jax import lax
from jax.experimental import pallas as pl
from jax.experimental.pallas import tpu as pltpu
from jax.sharding import PartitionSpec as P

STEPS = 4
INTERVALS = 2
BLOCK = 8
HALO = 2 * STEPS

COURANT = 0.35
FRICTION = 0.02
CORIOLIS = 0.3
GREEN_SCALE = 0.25
KEEP = 1.0 - FRICTION
HALF = 0.5 * COURANT

MESH = pl.DeviceIdType.MESH
F32 = jnp.float32
BF16 = jnp.bfloat16
DIRS = ((0, 1), (0, -1), (1, 0), (-1, 0), (1, 1), (1, -1), (-1, 1), (-1, -1))

SIDE = 8
SLOTS = 9


def iota(shape, dim):
    return lax.broadcasted_iota(jnp.int32, shape, dim)


def latitude(row_ids, row_count):
    return ((row_ids.astype(F32) + 0.5) / row_count - 0.5) * jnp.pi


def longitude(col_ids, col_count):
    return (col_ids.astype(F32) + 0.5) / col_count * (2.0 * jnp.pi)


def unit_vectors(lat_angle, lon_angle):
    cos_lat = jnp.cos(lat_angle)
    return (cos_lat * jnp.cos(lon_angle), cos_lat * jnp.sin(lon_angle), jnp.sin(lat_angle))


def lanes():
    return iota((8, 128), 1)


def pick(x, index):
    return jnp.take_along_axis(x, index, axis=1)


def exchange(values):
    lane = lanes()
    values = list(values)
    for bit in range(3):
        step = 1 << bit
        low = (lane & step) == 0
        index = lane ^ step
        for a in range(8):
            if a & step:
                continue
            b = a | step
            moved = pick(jnp.where(low, values[b], values[a]), index)
            values[a], values[b] = jnp.where(low, values[a], moved), jnp.where(low, moved, values[b])
    return values


def band(t):
    return pl.ds(BLOCK + t * BLOCK, BLOCK)


def shifted(t, by):
    return pl.ds(BLOCK + t * BLOCK + by, BLOCK)


def x_differences(values, with_side=True):
    lane = lanes()
    first, last = lane < 8, lane >= 120
    edge_east, edge_west = pltpu.roll(values[7], 8, 1), pltpu.roll(values[0], 120, 1)
    side = values[SIDE]
    left = [jnp.where(first, pltpu.roll(side, 8, 1), edge_east)] + values[:7]
    right = values[1:8] + [jnp.where(last, pltpu.roll(side, 120, 1), edge_west)]
    if with_side:
        left.append(jnp.where(first, edge_east, pltpu.roll(side, 16, 1)))
        right.append(jnp.where(last, edge_west, pltpu.roll(side, 112, 1)))
    return [r - l for l, r in zip(left, right)]


def move_flow(tiles, n, last, eta, p_in, q_in, p_out, q_out, depth, turn):
    for t in range(tiles):
        inner = not last or 0 < t < tiles - 1
        coriolis = turn[t]
        if inner:
            diff = x_differences([eta[j, band(t), :] for j in range(SLOTS)])
        for j in range(SLOTS if inner else SIDE):
            d = depth[n, j, t * BLOCK : (t + 1) * BLOCK, :]
            p, q = p_in[j, band(t), :], q_in[j, band(t), :]
            if inner:
                p_out[j, band(t), :] = p + coriolis * q - d * diff[j]
            north = eta[j, shifted(t, 1), :] - eta[j, shifted(t, -1), :]
            q_out[j, band(t), :] = q - coriolis * p - d * north


def surface_change(t, n, with_side, p, q, wet):
    diff = x_differences([p[j, band(t), :] for j in range(SLOTS)], with_side)
    return [
        wet[n, j, t * BLOCK : (t + 1) * BLOCK, :]
        * (diff[j] + (q[j, shifted(t, 1), :] - q[j, shifted(t, -1), :]))
        for j in range(SLOTS if with_side else SIDE)
    ]


def move_surface(tiles, n, eta_in, eta_out, p, q, wet):
    for t in range(tiles):
        change = surface_change(t, n, True, p, q, wet)
        for j in range(SLOTS):
            eta_out[j, band(t), :] = eta_in[j, band(t), :] - change[j]


def kernel(
    nx, ny, members, rows, cols,
    h_in, u_in, v_in, d_in, o_in,
    eta, pp, qq, depth1, wet1, turn, restore, fine, l_out,
    in3, in_d, in_o, strips, land, slab_out, slab, st, st_land, st_ns, base, depth0, wet0, green, tiles,
    in_sem, gs_sem, gr_sem, hs_sem, hr_sem, ss_sem, sr_sem,
):
    gx, gy = lax.axis_index("gx"), lax.axis_index("gy")
    n = nx * ny
    rb_own, cb_own = rows // BLOCK, cols // BLOCK
    per_device = rb_own * cb_own
    pair_rows = 2 * per_device
    coarse_rows, coarse_cols = rb_own * ny, cb_own * nx
    ext = rows + 2 * HALO
    ext_tiles = ext // BLOCK
    my_slot = ((gx // 2) * ny + gy) * 2 + gx % 2
    fields = (eta, pp, qq)

    inputs = [
        pltpu.make_async_copy(src, dst, in_sem.at[k])
        for k, (src, dst) in enumerate(
            ((d_in, in_d), (o_in, in_o), (h_in, in3.at[0]), (u_in, in3.at[1]), (v_in, in3.at[2]))
        )
    ]
    for copy in inputs:
        copy.start()

    def wrap(index, size):
        return jnp.where(index >= size, index - size, index)

    def to_all_others(fn):
        others = [wrap(gy + dy, ny) for dy in range(ny)]
        for y in others[1:]:
            fn({"gx": gx, "gy": y})

        def column(dx, carry):
            x = wrap(gx + dx, nx)
            for y in others:
                fn({"gx": x, "gy": y})
            return carry

        lax.fori_loop(1, nx, column, 0)

    barrier = pltpu.get_barrier_semaphore()

    to_all_others(
        lambda device: pl.semaphore_signal(barrier, inc=1, device_id=device, device_id_type=MESH)
    )

    def target_of(dx, dy):
        return {"gx": wrap(jnp.where(gx + dx < 0, gx + dx + nx, gx + dx), nx), "gy": gy + dy}

    def when(dy, sending, fn):
        if dy == 0:
            fn()
        else:
            beyond = gy + (dy if sending else -dy)
            pl.when((beyond >= 0) & (beyond < ny))(fn)

    def static_copy(k):
        dx, dy = DIRS[k]
        side = 0 if dx > 0 else 1
        if dy == 0:
            src, dst = st, st_land.at[side, pl.ds(HALO, rows)]
        else:
            src = st.at[pl.ds(rows - HALO if dy > 0 else 0, HALO)]
            at = 0 if dy > 0 else HALO + rows
            dst = st_ns.at[0 if dy > 0 else 1] if dx == 0 else st_land.at[side, pl.ds(at, HALO)]
        return pltpu.make_async_remote_copy(
            src_ref=src, dst_ref=dst, send_sem=ss_sem.at[k], recv_sem=sr_sem.at[k],
            device_id=target_of(dx, dy), device_id_type=MESH,
        )

    def halo_copy(i, k):
        dx, dy = DIRS[k]
        side = 0 if dx > 0 else 1
        if dx == 0:
            at = 0 if dy > 0 else 1
            src, dst = slab_out.at[i, at], slab.at[i, at]
        elif dy == 0:
            src, dst = strips.at[i], land.at[i, side, :, pl.ds(1, rb_own)]
        else:
            src = strips.at[i, :, pl.ds(rb_own - 1 if dy > 0 else 0, 1)]
            dst = land.at[i, side, :, pl.ds(0 if dy > 0 else ext_tiles - 1, 1)]
        return pltpu.make_async_remote_copy(
            src_ref=src, dst_ref=dst, send_sem=hs_sem.at[i, k], recv_sem=hr_sem.at[i, k],
            device_id=target_of(dx, dy), device_id_type=MESH,
        )

    def clear(side):
        at = 0 if side == 0 else ext_tiles - 1
        slab[:, side] = jnp.zeros_like(slab[:, side])
        land[:, :, :, at] = jnp.zeros_like(land[:, :, :, at])
        st_ns[side] = jnp.zeros_like(st_ns[side])
        st_land[:, at * BLOCK : (at + 1) * BLOCK] = jnp.zeros((2, HALO, cols), F32)

    pl.when(gy == 0)(lambda: clear(0))
    pl.when(gy == ny - 1)(lambda: clear(1))

    lane = lanes()
    sub = iota((8, 128), 0)

    def put_base(t, source, slots):
        for j in slots:
            base[j, t * BLOCK : (t + 1) * BLOCK, :] = pick(source, (lane & -8) + j)

    def send_loads(i, sums):
        spread = None
        for t, total in enumerate(sums):
            total = jnp.broadcast_to(jnp.sum(total, axis=0, keepdims=True), (8, 128)) * (1.0 / (BLOCK * HALF))
            mine = pick(total, (lane & 15) * 8 + sub)
            here = lane // cb_own == t + rb_own * (gx % 2)
            spread = jnp.where(here, mine, 0.0 if spread is None else spread)
        tiles[i, my_slot] = spread.astype(BF16)

    def pack(i, f):
        ref = fields[f]
        for at, t in enumerate((rb_own, 1)):
            for k in range(4):
                both = jnp.concatenate([ref[2 * k, band(t), :], ref[2 * k + 1, band(t), :]], axis=0)
                slab_out[i, at, f, k] = both.astype(BF16)
        packed = [None] * rb_own
        for j in range(8):
            index = (lane + (128 - 16 * j - 8)) & 127
            for b in range(rb_own):
                moved = pick(ref[j, band(b + 1), :], index)
                packed[b] = moved if j == 0 else jnp.where(lane // 16 == j, moved, packed[b])
        for b in range(rb_own):
            strips[i, f, b] = packed[b]

    def assemble(i):
        west = (lane & 8) != 0
        for f, ref in enumerate(fields):
            for t in range(ext_tiles):
                both = jnp.where(west, land[i, 1, f, t], land[i, 0, f, t])
                ref[SIDE, band(t), :] = pick(both, lane ^ 8)
            for at, t in enumerate((0, ext_tiles - 1)):
                for k in range(4):
                    both = slab[i, at, f, k].astype(F32)
                    ref[2 * k, band(t), :] = both[:8]
                    ref[2 * k + 1, band(t), :] = both[8:]

    def tables(first, depth, wet):
        def fill(t, carry):
            part = pl.ds(t * BLOCK, BLOCK)
            for j in range(SLOTS):
                d = base[j, part, :]
                w = jnp.where(d > 0.0, 1.0, 0.0)
                for k in range(STEPS):
                    depth[k, j, part, :] = d * KEEP ** -(first + k + 1)
                    wet[k, j, part, :] = w * KEEP ** (first + k + 1)
            return carry

        lax.fori_loop(0, ext_tiles, fill, 0)

    def start_interval(i):
        def send(device):
            pltpu.make_async_remote_copy(
                src_ref=tiles.at[i, my_slot], dst_ref=tiles.at[i, my_slot],
                send_sem=gs_sem.at[i], recv_sem=gr_sem.at[i],
                device_id=device, device_id_type=MESH,
            ).start()

        to_all_others(send)

    def start_halos(i):
        for k in range(len(DIRS)):
            when(DIRS[k][1], True, lambda k=k: halo_copy(i, k).start())

    def wait_halos(i):
        for k in range(len(DIRS)):
            when(DIRS[k][1], False, lambda k=k: halo_copy(i, k).wait_recv())

    def finish_sends(i):
        for k in range(len(DIRS)):
            when(DIRS[k][1], True, lambda k=k: halo_copy(i, k).wait_send())

    def everyone(i):
        return pltpu.make_async_remote_copy(
            src_ref=tiles.at[i, pl.ds(0, n - 1)], dst_ref=tiles.at[i, pl.ds(0, n - 1)],
            send_sem=gs_sem.at[i], recv_sem=gr_sem.at[i],
            device_id=target_of(1, 0), device_id_type=MESH,
        )

    def make_turning():
        for e in range(ext_tiles):
            row_ids = gy * rows - HALO + e * BLOCK + iota((BLOCK, cols), 0)
            turn[e] = (CORIOLIS / KEEP) * jnp.sin(latitude(row_ids, rows * ny))

    def make_green():
        t = iota((8, 128), 1)
        north = per_device
        south = north + cb_own
        west = south + cb_own
        east = west + rb_own + 2
        t_row = jnp.where(t < north, t // cb_own, jnp.where(t < south, -1, rb_own))
        t_col = jnp.where(t < north, t % cb_own, jnp.where(t < south, t - north, t - south))
        t_row = jnp.where(t >= east, t - east - 1, jnp.where(t >= west, t - west - 1, t_row))
        t_col = jnp.where(t >= east, cb_own, jnp.where(t >= west, -1, t_col))
        t_row = gy * rb_own + t_row
        t_col = gx * cb_own + t_col
        t_col = jnp.where(t_col < 0, t_col + coarse_cols, t_col)
        t_col = jnp.where(t_col >= coarse_cols, t_col - coarse_cols, t_col)
        target = unit_vectors(latitude(t_row, coarse_rows), longitude(t_col, coarse_cols))
        target = [jnp.broadcast_to(x[:1], (pair_rows, 128)) for x in target]

        def green_group(g, carry):
            p = g * 8 + iota((8, pair_rows), 0)
            k = iota((8, pair_rows), 1)
            s_col = ((p // ny) * 2 + k // per_device) * cb_own + k % cb_own
            s_row = (p % ny) * rb_own + (k % per_device) // cb_own
            source = unit_vectors(latitude(s_row, coarse_rows), longitude(s_col, coarse_cols))
            source = [jnp.transpose(x) for x in source]
            for j in range(8):
                square = None
                for s, t_vec in zip(source, target):
                    diff = jnp.broadcast_to(s[:, j : j + 1], (pair_rows, 128)) - t_vec
                    square = diff * diff if square is None else square + diff * diff
                value = GREEN_SCALE / (1.0 + jnp.sqrt(square) * (coarse_rows / math.pi))
                green[g * 8 + j] = value.astype(BF16)
            return carry

        lax.fori_loop(0, n // 16, green_group, 0)

    def finish_base():
        scale = HALF * HALF
        for t, side in ((0, 0), (ext_tiles - 1, 1)):
            put_base(t, st_ns[side] * scale, range(8))
        for t in range(ext_tiles):
            part = slice(t * BLOCK, (t + 1) * BLOCK)
            east = pick(st_land[1, part], lane // 16)
            west = pick(st_land[0, part], lane // 16 + (cols - 8))
            base[SIDE, part, :] = jnp.where((lane & 8) != 0, west, east) * scale

    def load(i):
        group = 16 if n // 2 % 16 == 0 else 1

        def add_group(g, total):
            for j in range(group):
                p = g * group + j
                tile = tiles[i, 2 * p].astype(F32) + tiles[i, 2 * p + 1].astype(F32)
                total = total + jnp.dot(tile.astype(BF16), green[p], preferred_element_type=F32)
            return total

        loading = lax.fori_loop(0, n // 2 // group, add_group, jnp.zeros((members, 128), F32))
        l_out[...] = loading
        loading = loading * HALF
        north = per_device
        south = north + cb_own
        west = south + cb_own
        east = west + rb_own + 2
        own_member = (lane & 7) == sub
        for t in range(ext_tiles):
            first = north if t == 0 else south if t == ext_tiles - 1 else (t - 1) * cb_own
            main = pick(loading, lane // 8 + first)
            side = pick(loading, jnp.where((lane & 8) != 0, west + t, east + t))
            both = []
            for value in (main, side):
                value = jnp.where(own_member, value, 0.0)
                if t == 0:
                    value = jnp.where(gy == 0, 0.0, value)
                if t == ext_tiles - 1:
                    value = jnp.where(gy == ny - 1, 0.0, value)
                both.append(jnp.broadcast_to(jnp.sum(value, axis=0, keepdims=True), (8, 128)))
            fine[t] = both[0]
            for j in range(8):
                eta[j, band(t), :] = eta[j, band(t), :] - both[0]
            eta[SIDE, band(t), :] = eta[SIDE, band(t), :] - both[1]

    def interval(i):
        def step(n, carry):
            move_flow(ext_tiles, n, False, eta, pp, qq, pp, qq, depth0, turn)
            move_surface(ext_tiles, n, eta, eta, pp, qq, wet0)
            return carry

        lax.fori_loop(0, STEPS - 1, step, 0)
        move_flow(ext_tiles, STEPS - 1, True, eta, pp, qq, pp, qq, depth0, turn)
        sums = []
        for t in range(1, ext_tiles - 1):
            change = surface_change(t, STEPS - 1, False, pp, qq, wet0)
            total = None
            for j in range(8):
                value = eta[j, band(t), :] - change[j] + fine[t]
                eta[j, band(t), :] = value
                value = value * wet0[STEPS - 1, j, t * BLOCK : (t + 1) * BLOCK, :]
                total = value if total is None else total + value
            sums.append(total * KEEP ** -STEPS)
        return sums

    for copy in inputs[:3]:
        copy.wait()
    st[...] = jnp.where(in_o[...] > 0, in_d[...], 0.0)
    sums = []
    for t in range(1, ext_tiles - 1):
        part = slice((t - 1) * BLOCK, t * BLOCK)
        put_base(t, st[part, :] * (HALF * HALF), range(8))
        total = None
        for j, value in enumerate(exchange([in3[0, m, part, :] for m in range(8)])):
            value = value * HALF
            eta[j, band(t), :] = value
            value = jnp.where(base[j, t * BLOCK : (t + 1) * BLOCK, :] > 0.0, value, 0.0)
            total = value if total is None else total + value
        sums.append(total)
    send_loads(0, sums)
    for copy in inputs[3:]:
        copy.wait()
    for f in (1, 2):
        for t in range(1, ext_tiles - 1):
            part = slice((t - 1) * BLOCK, t * BLOCK)
            for j, value in enumerate(exchange([in3[f, m, part, :] for m in range(8)])):
                fields[f][j, band(t), :] = value * base[j, t * BLOCK : (t + 1) * BLOCK, :]
    for f in range(3):
        pack(0, f)
    pl.semaphore_wait(barrier, n - 1)
    start_interval(0)
    for k, (dx, dy) in enumerate(DIRS):
        when(dy, True, lambda k=k: static_copy(k).start())
    start_halos(0)

    make_turning()
    make_green()
    for k, (dx, dy) in enumerate(DIRS):
        when(dy, False, lambda k=k: static_copy(k).wait_recv())
    finish_base()
    tables(0, depth0, wet0)
    wait_halos(0)
    assemble(0)
    everyone(0).wait_recv()
    load(0)
    send_loads(1, interval(0))
    start_interval(1)
    for f in range(3):
        pack(1, f)
    start_halos(1)
    tables(STEPS, depth1, wet1)
    for j in range(8):
        d = base[j, BLOCK : BLOCK + rows, :]
        restore[j] = jnp.where(d > 0.0, KEEP ** (2 * STEPS) / jnp.where(d > 0.0, d, 1.0), 0.0)
    for k, (dx, dy) in enumerate(DIRS):
        when(dy, True, lambda k=k: static_copy(k).wait_send())
    everyone(0).wait_send()
    finish_sends(0)
    wait_halos(1)
    assemble(1)
    everyone(1).wait_recv()
    load(1)
    finish_sends(1)
    everyone(1).wait_send()


def finish(
    members, rows, cols,
    eta_in, p_in, q_in, depth, wet, turn, restore, fine, l_in,
    h_out, u_out, v_out, l_out,
    eta, pp, qq, staged, l_staged, sem,
):
    ext_tiles = (rows + 2 * HALO) // BLOCK
    blocks, width = l_staged.shape[1:]
    for b in range(blocks):
        l_staged[:, b, :] = l_in[:, b * width : (b + 1) * width]
    l_copy = pltpu.make_async_copy(l_staged, l_out, sem.at[3])
    l_copy.start()

    move_flow(ext_tiles, 0, False, eta_in, p_in, q_in, pp, qq, depth, turn)
    move_surface(ext_tiles, 0, eta_in, eta, pp, qq, wet)

    def step(n, carry):
        move_flow(ext_tiles, n, False, eta, pp, qq, pp, qq, depth, turn)
        move_surface(ext_tiles, n, eta, eta, pp, qq, wet)
        return carry

    lax.fori_loop(1, STEPS - 1, step, 0)
    move_flow(ext_tiles, STEPS - 1, True, eta, pp, qq, pp, qq, depth, turn)
    copies = [pltpu.make_async_copy(staged.at[f], out, sem.at[f]) for f, out in enumerate((h_out, u_out, v_out))]

    def place(f, t, values):
        for m, value in enumerate(exchange(values)):
            staged[f, m, (t - 1) * BLOCK : t * BLOCK, :] = value

    for f, ref in ((1, pp), (2, qq)):
        for t in range(1, ext_tiles - 1):
            part = slice((t - 1) * BLOCK, t * BLOCK)
            place(f, t, [ref[j, band(t), :] * restore[j, part, :] for j in range(8)])
        copies[f].start()
    for t in range(1, ext_tiles - 1):
        change = surface_change(t, STEPS - 1, False, pp, qq, wet)
        place(0, t, [(eta[j, band(t), :] - change[j] + fine[t]) * (1.0 / HALF) for j in range(8)])
    copies[0].start()
    for copy in copies:
        copy.wait()
    l_copy.wait()


def shards(nx, ny, elevation, east_velocity, north_velocity, water_depth, land_sea):
    members, rows, cols = elevation.shape
    rb_own, cb_own = rows // BLOCK, cols // BLOCK
    n = nx * ny
    ext = rows + 2 * HALO
    tiles = ext // BLOCK
    hbm_spec = pl.BlockSpec(memory_space=pltpu.HBM)
    vmem_spec = pl.BlockSpec(memory_space=pltpu.VMEM)
    dma = pltpu.SemaphoreType.DMA
    field = (SLOTS, ext + 2 * BLOCK, cols)
    table = (STEPS, SLOTS, ext, cols)
    shape = (members, rows, cols)
    outs = tuple(
        jax.ShapeDtypeStruct(s, F32)
        for s in (
            field, field, field, table, table, (tiles, BLOCK, cols), (8, rows, cols), (tiles, BLOCK, cols),
            (members, 128),
        )
    )
    state = pl.pallas_call(
        functools.partial(kernel, nx, ny, members, rows, cols),
        out_shape=outs,
        in_specs=[hbm_spec] * 5,
        out_specs=(vmem_spec,) * len(outs),
        scratch_shapes=[
            pltpu.VMEM((3,) + shape, F32),
            pltpu.VMEM((rows, cols), F32),
            pltpu.VMEM((rows, cols), jnp.int32),
            pltpu.VMEM((INTERVALS, 3, rb_own, 8, cols), F32),
            pltpu.VMEM((INTERVALS, 2, 3, tiles, 8, cols), F32),
            pltpu.VMEM((INTERVALS, 2, 3, 4, 16, cols), BF16),
            pltpu.VMEM((INTERVALS, 2, 3, 4, 16, cols), BF16),
            pltpu.VMEM((rows, cols), F32),
            pltpu.VMEM((2, ext, cols), F32),
            pltpu.VMEM((2, HALO, cols), F32),
            pltpu.VMEM((SLOTS, ext, cols), F32),
            pltpu.VMEM(table, F32),
            pltpu.VMEM(table, F32),
            pltpu.VMEM((n // 2, 2 * rb_own * cb_own, 128), BF16),
            pltpu.VMEM((INTERVALS, n, members, 2 * rb_own * cb_own), BF16),
            dma((5,)),
            dma((INTERVALS,)),
            dma((INTERVALS,)),
            dma((INTERVALS, len(DIRS))),
            dma((INTERVALS, len(DIRS))),
            dma((len(DIRS),)),
            dma((len(DIRS),)),
        ],
        compiler_params=pltpu.CompilerParams(
            collective_id=0, has_side_effects=True, vmem_limit_bytes=40 * 1024 * 1024
        ),
        name="tide",
    )(
        *(
            pltpu.with_memory_space_constraint(x, pltpu.HBM)
            for x in (elevation, east_velocity, north_velocity, water_depth, land_sea)
        )
    )
    coarse = jax.ShapeDtypeStruct((members, rb_own, cb_own), F32)
    whole = jax.ShapeDtypeStruct(shape, F32)
    return pl.pallas_call(
        functools.partial(finish, members, rows, cols),
        out_shape=(whole, whole, whole, coarse),
        in_specs=[vmem_spec] * len(outs),
        out_specs=(hbm_spec,) * 4,
        scratch_shapes=[
            pltpu.VMEM(field, F32),
            pltpu.VMEM(field, F32),
            pltpu.VMEM(field, F32),
            pltpu.VMEM((3,) + shape, F32),
            pltpu.VMEM(coarse.shape, F32),
            dma((4,)),
        ],
        compiler_params=pltpu.CompilerParams(vmem_limit_bytes=8 * 1024 * 1024),
        name="finish",
    )(*state)


def solution(mesh):
    nx, ny = mesh.shape["gx"], mesh.shape["gy"]
    tile = P(None, "gy", "gx")
    return jax.shard_map(
        functools.partial(shards, nx, ny),
        mesh=mesh,
        in_specs=(tile, tile, tile, P("gy", "gx"), P("gy", "gx")),
        out_specs=(tile, tile, tile, tile),
        check_vma=False,
    )
```

profile of v0, /device:TPU:0, one launch (start us, length us, event | category | flops | bytes accessed | tf_op | source)
XLA Modules:
  0.0 22.8 jit_solution(9580302669628727550)
XLA Ops:
  0.6 20.2 %tide.1 = (f32[9,64,128]{2,1,0:T(8,128)S(1)}, f32[9,64,128]{2,1,0:T(8,128)S(1)}, f32[9,64,128]{2,1,0:T(8,128)S(1)}, f32[4,9,48,128]{3,2,1,0:T(8,128)S(1)}, f32[4...) custom-call(f32[8,32,128]{2,1,0:T(8,128)} %h_in.1, ...), custom_call_target="tpu_custom_call" | custom-call | tf_op jit(solution)/shard_map/tide/pallas_call | solution.py:537
  20.8 1.9 %finish.1 = (f32[8,32,128]{2,1,0:T(8,128)}, f32[8,32,128]{2,1,0:T(8,128)}, f32[8,32,128]{2,1,0:T(8,128)}, f32[8,4,16]{2,1,0:T(4,128)}) custom-call(f32[9,64,128]{2,1,0:T(8,128)S(1)} %get-tuple-element.13.eta_in, f32[9,64,128]{2,1,0:T(8,128)S(1)} %get-tuple-element.14.p_in, f32[9,64,128]{2,1,0:T(8,128)S(1)} %get-tuple-element.15.q_in, ...), custom_call_target="tpu_custom_call" | custom-call | tf_op jit(solution)/shard_map/finish/pallas_call | solution.py:578
where the time goes:
time: 23 us; the launch traced here: 22.8 us
  Pallas kernels  22.1 us (96%)
  between operations  0.64 us (3%)
    pallas_call x1, Pallas kernels, shards(): pl.pallas_call(functools.partial(kernel, nx, ny, members, rows, cols), ou...  20.2 us
    pallas_call x1, Pallas kernels, shards(): pl.pallas_call(functools.partial(finish, members, rows, cols), out_shape=...  1.92 us

commit v1 on v0

--- a/solution.py
+++ b/solution.py
@@ -23,7 +23,6 @@
 MESH = pl.DeviceIdType.MESH
 F32 = jnp.float32
 BF16 = jnp.bfloat16
-DIRS = ((0, 1), (0, -1), (1, 0), (-1, 0), (1, 1), (1, -1), (-1, 1), (-1, -1))
 
 SIDE = 8
 SLOTS = 9
@@ -126,8 +125,8 @@
     nx, ny, members, rows, cols,
     h_in, u_in, v_in, d_in, o_in,
     eta, pp, qq, depth1, wet1, turn, restore, fine, l_out,
-    in3, in_d, in_o, strips, land, slab_out, slab, st, st_land, st_ns, base, depth0, wet0, green, tiles,
-    in_sem, gs_sem, gr_sem, hs_sem, hr_sem, ss_sem, sr_sem,
+    in3, in_d, in_o, strips, land, slab_out, slab, counted, st, base, depth0, wet0, green, tiles,
+    in_sem, gs_sem, gr_sem, hs_sem, hr_sem,
 ):
     gx, gy = lax.axis_index("gx"), lax.axis_index("gy")
     n = nx * ny
@@ -181,42 +180,41 @@
             beyond = gy + (dy if sending else -dy)
             pl.when((beyond >= 0) & (beyond < ny))(fn)
 
-    def static_copy(k):
-        dx, dy = DIRS[k]
-        side = 0 if dx > 0 else 1
-        if dy == 0:
-            src, dst = st, st_land.at[side, pl.ds(HALO, rows)]
-        else:
-            src = st.at[pl.ds(rows - HALO if dy > 0 else 0, HALO)]
-            at = 0 if dy > 0 else HALO + rows
-            dst = st_ns.at[0 if dy > 0 else 1] if dx == 0 else st_land.at[side, pl.ds(at, HALO)]
+    planes, layers = (5, 3), (13, 12)
+
+    def remote(src, dst, i, group, dx, dy):
         return pltpu.make_async_remote_copy(
-            src_ref=src, dst_ref=dst, send_sem=ss_sem.at[k], recv_sem=sr_sem.at[k],
+            src_ref=src, dst_ref=dst, send_sem=hs_sem.at[i, group], recv_sem=hr_sem.at[i, group],
             device_id=target_of(dx, dy), device_id_type=MESH,
         )
 
-    def halo_copy(i, k):
-        dx, dy = DIRS[k]
-        side = 0 if dx > 0 else 1
-        if dx == 0:
-            at = 0 if dy > 0 else 1
-            src, dst = slab_out.at[i, at], slab.at[i, at]
-        elif dy == 0:
-            src, dst = strips.at[i], land.at[i, side, :, pl.ds(1, rb_own)]
-        else:
-            src = strips.at[i, :, pl.ds(rb_own - 1 if dy > 0 else 0, 1)]
-            dst = land.at[i, side, :, pl.ds(0 if dy > 0 else ext_tiles - 1, 1)]
-        return pltpu.make_async_remote_copy(
-            src_ref=src, dst_ref=dst, send_sem=hs_sem.at[i, k], recv_sem=hr_sem.at[i, k],
-            device_id=target_of(dx, dy), device_id_type=MESH,
+    def beside(i, dx):
+        part = pl.ds(0, planes[i])
+        return remote(
+            strips.at[i, :, part], land.at[i, 0 if dx > 0 else 1, pl.ds(1, rb_own), part], i, 0, dx, 0
         )
+
+    def beside_all(i):
+        both = land.at[i, :, pl.ds(1, rb_own), pl.ds(0, planes[i])]
+        return remote(both, both, i, 0, 1, 0)
+
+    def start_beyond(i, dy):
+        at, group = (0, 1) if dy > 0 else (1, 2)
+        part, rest = pl.ds(0, planes[i]), pl.ds(0, layers[i])
+        remote(slab_out.at[i, at, rest], slab.at[i, at, rest], i, group, 0, dy).start()
+        for dx in (1, -1):
+            src = strips.at[i, pl.ds(rb_own - 1 if dy > 0 else 0, 1), part]
+            dst = land.at[i, 0 if dx > 0 else 1, pl.ds(0 if dy > 0 else ext_tiles - 1, 1), part]
+            remote(src, dst, i, group, dx, dy).start()
+
+    def beyond_all(i, dy):
+        every = counted.at[pl.ds(0, layers[i] + planes[i])]
+        return remote(every, every, i, 1 if dy > 0 else 2, 1, 0)
 
     def clear(side):
         at = 0 if side == 0 else ext_tiles - 1
         slab[:, side] = jnp.zeros_like(slab[:, side])
-        land[:, :, :, at] = jnp.zeros_like(land[:, :, :, at])
-        st_ns[side] = jnp.zeros_like(st_ns[side])
-        st_land[:, at * BLOCK : (at + 1) * BLOCK] = jnp.zeros((2, HALO, cols), F32)
+        land[:, :, at] = jnp.zeros_like(land[:, :, at])
 
     pl.when(gy == 0)(lambda: clear(0))
     pl.when(gy == ny - 1)(lambda: clear(1))
@@ -226,7 +224,7 @@
 
     def put_base(t, source, slots):
         for j in slots:
-            base[j, t * BLOCK : (t + 1) * BLOCK, :] = pick(source, (lane & -8) + j)
+            base[j, band(t), :] = pick(source, (lane & -8) + j)
 
     def send_loads(i, sums):
         spread = None
@@ -237,12 +235,20 @@
             spread = jnp.where(here, mine, 0.0 if spread is None else spread)
         tiles[i, my_slot] = spread.astype(BF16)
 
+    def two_parts(x):
+        high = x.astype(BF16).astype(F32)
+        return high, x - high
+
     def pack(i, f):
-        ref = fields[f]
+        ref = (*fields, base)[f]
         for at, t in enumerate((rb_own, 1)):
+            if f == 3:
+                edge = two_parts(st[(t - 1) * BLOCK : t * BLOCK, :] * (HALF * HALF))
+                slab_out[i, at, 12] = jnp.concatenate(edge, axis=0).astype(BF16)
+                continue
             for k in range(4):
                 both = jnp.concatenate([ref[2 * k, band(t), :], ref[2 * k + 1, band(t), :]], axis=0)
-                slab_out[i, at, f, k] = both.astype(BF16)
+                slab_out[i, at, 4 * f + k] = both.astype(BF16)
         packed = [None] * rb_own
         for j in range(8):
             index = (lane + (128 - 16 * j - 8)) & 127
@@ -250,32 +256,52 @@
                 moved = pick(ref[j, band(b + 1), :], index)
                 packed[b] = moved if j == 0 else jnp.where(lane // 16 == j, moved, packed[b])
         for b in range(rb_own):
-            strips[i, f, b] = packed[b]
+            parts = two_parts(packed[b]) if f == 3 else (packed[b],)
+            for k, part in enumerate(parts):
+                strips[i, b, f + k] = part.astype(BF16)
+
+    def side_of(i, t, planes):
+        west, east = (sum(land[i, side, t, k].astype(F32) for k in planes) for side in (0, 1))
+        return pick(jnp.where((lane & 8) != 0, east, west), lane ^ 8)
 
     def assemble(i):
-        west = (lane & 8) != 0
         for f, ref in enumerate(fields):
             for t in range(ext_tiles):
-                both = jnp.where(west, land[i, 1, f, t], land[i, 0, f, t])
-                ref[SIDE, band(t), :] = pick(both, lane ^ 8)
+                ref[SIDE, band(t), :] = side_of(i, t, (f,))
             for at, t in enumerate((0, ext_tiles - 1)):
                 for k in range(4):
-                    both = slab[i, at, f, k].astype(F32)
+                    both = slab[i, at, 4 * f + k].astype(F32)
                     ref[2 * k, band(t), :] = both[:8]
                     ref[2 * k + 1, band(t), :] = both[8:]
 
-    def tables(first, depth, wet):
+    def finish_base():
+        for at, t in enumerate((0, ext_tiles - 1)):
+            both = slab[0, at, 12].astype(F32)
+            put_base(t, both[:8] + both[8:], range(8))
+        for t in range(ext_tiles):
+            base[SIDE, band(t), :] = side_of(0, t, (3, 4))
+
+    def table(j, t, first, depth, wet):
+        d = base[j, band(t), :]
+        w = jnp.where(d > 0.0, 1.0, 0.0)
+        part = pl.ds(t * BLOCK, BLOCK)
+        for k in range(STEPS):
+            depth[k, j, part, :] = d * KEEP ** -(first + k + 1)
+            wet[k, j, part, :] = w * KEEP ** (first + k + 1)
+
+    def own_tables(first, depth, wet):
         def fill(t, carry):
-            part = pl.ds(t * BLOCK, BLOCK)
-            for j in range(SLOTS):
-                d = base[j, part, :]
-                w = jnp.where(d > 0.0, 1.0, 0.0)
-                for k in range(STEPS):
-                    depth[k, j, part, :] = d * KEEP ** -(first + k + 1)
-                    wet[k, j, part, :] = w * KEEP ** (first + k + 1)
+            for j in range(8):
+                table(j, t, first, depth, wet)
             return carry
 
-        lax.fori_loop(0, ext_tiles, fill, 0)
+        lax.fori_loop(1, ext_tiles - 1, fill, 0)
+
+    def edge_tables(first, depth, wet):
+        for t in range(ext_tiles):
+            for j in range(8) if t in (0, ext_tiles - 1) else ():
+                table(j, t, first, depth, wet)
+            table(SIDE, t, first, depth, wet)
 
     def start_interval(i):
         def send(device):
@@ -288,16 +314,20 @@
         to_all_others(send)
 
     def start_halos(i):
-        for k in range(len(DIRS)):
-            when(DIRS[k][1], True, lambda k=k: halo_copy(i, k).start())
+        for dx in (1, -1):
+            beside(i, dx).start()
+        for dy in (1, -1):
+            when(dy, True, lambda dy=dy: start_beyond(i, dy))
 
     def wait_halos(i):
-        for k in range(len(DIRS)):
-            when(DIRS[k][1], False, lambda k=k: halo_copy(i, k).wait_recv())
+        beside_all(i).wait_recv()
+        for dy in (1, -1):
+            when(dy, False, lambda dy=dy: beyond_all(i, dy).wait_recv())
 
     def finish_sends(i):
-        for k in range(len(DIRS)):
-            when(DIRS[k][1], True, lambda k=k: halo_copy(i, k).wait_send())
+        beside_all(i).wait_send()
+        for dy in (1, -1):
+            when(dy, True, lambda dy=dy: beyond_all(i, dy).wait_send())
 
     def everyone(i):
         return pltpu.make_async_remote_copy(
@@ -346,27 +376,25 @@
 
         lax.fori_loop(0, n // 16, green_group, 0)
 
-    def finish_base():
-        scale = HALF * HALF
-        for t, side in ((0, 0), (ext_tiles - 1, 1)):
-            put_base(t, st_ns[side] * scale, range(8))
-        for t in range(ext_tiles):
-            part = slice(t * BLOCK, (t + 1) * BLOCK)
-            east = pick(st_land[1, part], lane // 16)
-            west = pick(st_land[0, part], lane // 16 + (cols - 8))
-            base[SIDE, part, :] = jnp.where((lane & 8) != 0, west, east) * scale
-
     def load(i):
-        group = 16 if n // 2 % 16 == 0 else 1
+        half = n // 4
+        group = math.gcd(8, half)
+
+        def pair(p):
+            return tiles[i, 2 * p].astype(F32) + tiles[i, 2 * p + 1].astype(F32)
 
         def add_group(g, total):
-            for j in range(group):
-                p = g * group + j
-                tile = tiles[i, 2 * p].astype(F32) + tiles[i, 2 * p + 1].astype(F32)
-                total = total + jnp.dot(tile.astype(BF16), green[p], preferred_element_type=F32)
-            return total
-
-        loading = lax.fori_loop(0, n // 2 // group, add_group, jnp.zeros((members, 128), F32))
+            left, right = [], []
+            for k in range(group):
+                q = g * group + k
+                left.append(jnp.concatenate([pair(q), pair(q + half)], axis=0).astype(BF16))
+                right.append(jnp.concatenate([green[q], green[q + half]], axis=1))
+            return total + jnp.dot(
+                jnp.concatenate(left, axis=1), jnp.concatenate(right, axis=0), preferred_element_type=F32
+            )
+
+        both = lax.fori_loop(0, half // group, add_group, jnp.zeros((2 * members, 256), F32))
+        loading = both[:members, :128] + both[members:, 128:]
         l_out[...] = loading
         loading = loading * HALF
         north = per_device
@@ -422,7 +450,7 @@
         for j, value in enumerate(exchange([in3[0, m, part, :] for m in range(8)])):
             value = value * HALF
             eta[j, band(t), :] = value
-            value = jnp.where(base[j, t * BLOCK : (t + 1) * BLOCK, :] > 0.0, value, 0.0)
+            value = jnp.where(base[j, band(t), :] > 0.0, value, 0.0)
             total = value if total is None else total + value
         sums.append(total)
     send_loads(0, sums)
@@ -432,23 +460,20 @@
         for t in range(1, ext_tiles - 1):
             part = slice((t - 1) * BLOCK, t * BLOCK)
             for j, value in enumerate(exchange([in3[f, m, part, :] for m in range(8)])):
-                fields[f][j, band(t), :] = value * base[j, t * BLOCK : (t + 1) * BLOCK, :]
-    for f in range(3):
+                fields[f][j, band(t), :] = value * base[j, band(t), :]
+    for f in range(4):
         pack(0, f)
     pl.semaphore_wait(barrier, n - 1)
     start_interval(0)
-    for k, (dx, dy) in enumerate(DIRS):
-        when(dy, True, lambda k=k: static_copy(k).start())
     start_halos(0)
 
     make_turning()
     make_green()
-    for k, (dx, dy) in enumerate(DIRS):
-        when(dy, False, lambda k=k: static_copy(k).wait_recv())
-    finish_base()
-    tables(0, depth0, wet0)
+    own_tables(0, depth0, wet0)
     wait_halos(0)
     assemble(0)
+    finish_base()
+    edge_tables(0, depth0, wet0)
     everyone(0).wait_recv()
     load(0)
     send_loads(1, interval(0))
@@ -456,12 +481,11 @@
     for f in range(3):
         pack(1, f)
     start_halos(1)
-    tables(STEPS, depth1, wet1)
+    own_tables(STEPS, depth1, wet1)
+    edge_tables(STEPS, depth1, wet1)
     for j in range(8):
-        d = base[j, BLOCK : BLOCK + rows, :]
+        d = base[j, 2 * BLOCK : 2 * BLOCK + rows, :]
         restore[j] = jnp.where(d > 0.0, KEEP ** (2 * STEPS) / jnp.where(d > 0.0, d, 1.0), 0.0)
-    for k, (dx, dy) in enumerate(DIRS):
-        when(dy, True, lambda k=k: static_copy(k).wait_send())
     everyone(0).wait_send()
     finish_sends(0)
     wait_halos(1)
@@ -495,7 +519,10 @@
 
     lax.fori_loop(1, STEPS - 1, step, 0)
     move_flow(ext_tiles, STEPS - 1, True, eta, pp, qq, pp, qq, depth, turn)
-    copies = [pltpu.make_async_copy(staged.at[f], out, sem.at[f]) for f, out in enumerate((h_out, u_out, v_out))]
+    copies = [pltpu.make_async_copy(staged.at[f], out, sem.at[f]) for f, out in ((1, u_out), (2, v_out))]
+    for t in range(rows // BLOCK):
+        part = pl.ds(t * BLOCK, BLOCK)
+        copies.append(pltpu.make_async_copy(staged.at[0, :, part], h_out.at[:, part], sem.at[4 + t]))
 
     def place(f, t, values):
         for m, value in enumerate(exchange(values)):
@@ -505,11 +532,11 @@
         for t in range(1, ext_tiles - 1):
             part = slice((t - 1) * BLOCK, t * BLOCK)
             place(f, t, [ref[j, band(t), :] * restore[j, part, :] for j in range(8)])
-        copies[f].start()
+        copies[f - 1].start()
     for t in range(1, ext_tiles - 1):
         change = surface_change(t, STEPS - 1, False, pp, qq, wet)
         place(0, t, [(eta[j, band(t), :] - change[j] + fine[t]) * (1.0 / HALF) for j in range(8)])
-    copies[0].start()
+        copies[1 + t].start()
     for copy in copies:
         copy.wait()
     l_copy.wait()
@@ -543,14 +570,13 @@
             pltpu.VMEM((3,) + shape, F32),
             pltpu.VMEM((rows, cols), F32),
             pltpu.VMEM((rows, cols), jnp.int32),
-            pltpu.VMEM((INTERVALS, 3, rb_own, 8, cols), F32),
-            pltpu.VMEM((INTERVALS, 2, 3, tiles, 8, cols), F32),
-            pltpu.VMEM((INTERVALS, 2, 3, 4, 16, cols), BF16),
-            pltpu.VMEM((INTERVALS, 2, 3, 4, 16, cols), BF16),
+            pltpu.VMEM((INTERVALS, rb_own, 5, 8, cols), BF16),
+            pltpu.VMEM((INTERVALS, 2, tiles, 5, 8, cols), BF16),
+            pltpu.VMEM((INTERVALS, 2, 13, 16, cols), BF16),
+            pltpu.VMEM((INTERVALS, 2, 13, 16, cols), BF16),
+            pltpu.VMEM((18, 16, cols), BF16),
             pltpu.VMEM((rows, cols), F32),
-            pltpu.VMEM((2, ext, cols), F32),
-            pltpu.VMEM((2, HALO, cols), F32),
-            pltpu.VMEM((SLOTS, ext, cols), F32),
+            pltpu.VMEM(field, F32),
             pltpu.VMEM(table, F32),
             pltpu.VMEM(table, F32),
             pltpu.VMEM((n // 2, 2 * rb_own * cb_own, 128), BF16),
@@ -558,10 +584,8 @@
             dma((5,)),
             dma((INTERVALS,)),
             dma((INTERVALS,)),
-            dma((INTERVALS, len(DIRS))),
-            dma((INTERVALS, len(DIRS))),
-            dma((len(DIRS),)),
-            dma((len(DIRS),)),
+            dma((INTERVALS, 3)),
+            dma((INTERVALS, 3)),
         ],
         compiler_params=pltpu.CompilerParams(
             collective_id=0, has_side_effects=True, vmem_limit_bytes=40 * 1024 * 1024
@@ -586,7 +610,7 @@
             pltpu.VMEM(field, F32),
             pltpu.VMEM((3,) + shape, F32),
             pltpu.VMEM(coarse.shape, F32),
-            dma((4,)),
+            dma((4 + rb_own,)),
         ],
         compiler_params=pltpu.CompilerParams(vmem_limit_bytes=8 * 1024 * 1024),
         name="finish",

time: 23 us -> 22 us (0.957)
  Pallas kernels: 22.1 us -> 21.1 us
    pallas_call x1, Pallas kernels: 20.2 us -> 19.2 us  [shards(): pl.pallas_call(functools.partial(kernel, nx, ny, members, rows, cols), ou...]
where the time goes in v1:
time: 22 us; the launch traced here: 21.8 us
  Pallas kernels  21.1 us (96%)
  between operations  0.64 us (3%)
    pallas_call x1, Pallas kernels, shards(): pl.pallas_call(functools.partial(kernel, nx, ny, members, rows, cols), ou...  19.2 us
    pallas_call x1, Pallas kernels, shards(): pl.pallas_call(functools.partial(finish, members, rows, cols), out_shape=...  1.94 us

profile of v1, /device:TPU:0, one launch (start us, length us, event | category | flops | bytes accessed | tf_op | source)
XLA Modules:
  0.0 21.8 jit_solution(17891802711773321136)
XLA Ops:
  0.6 19.2 %tide.1 = (f32[9,64,128]{2,1,0:T(8,128)S(1)}, f32[9,64,128]{2,1,0:T(8,128)S(1)}, f32[9,64,128]{2,1,0:T(8,128)S(1)}, f32[4,9,48,128]{3,2,1,0:T(8,128)S(1)}, f32[4...) custom-call(f32[8,32,128]{2,1,0:T(8,128)} %h_in.1, ...), custom_call_target="tpu_custom_call" | custom-call | tf_op jit(solution)/shard_map/tide/pallas_call | solution.py:564
  19.8 1.9 %finish.1 = (f32[8,32,128]{2,1,0:T(8,128)}, f32[8,32,128]{2,1,0:T(8,128)}, f32[8,32,128]{2,1,0:T(8,128)}, f32[8,4,16]{2,1,0:T(4,128)}) custom-call(f32[9,64,128]{2,1,0:T(8,128)S(1)} %get-tuple-element.13.eta_in, f32[9,64,128]{2,1,0:T(8,128)S(1)} %get-tuple-element.14.p_in, f32[9,64,128]{2,1,0:T(8,128)S(1)} %get-tuple-element.15.q_in, ...), custom_call_target="tpu_custom_call" | custom-call | tf_op jit(solution)/shard_map/finish/pallas_call | solution.py:602

commit v2 on v1

--- a/solution.py
+++ b/solution.py
@@ -125,7 +125,7 @@
     nx, ny, members, rows, cols,
     h_in, u_in, v_in, d_in, o_in,
     eta, pp, qq, depth1, wet1, turn, restore, fine, l_out,
-    in3, in_d, in_o, strips, land, slab_out, slab, counted, st, base, depth0, wet0, green, tiles,
+    in3, in_d, in_o, strips, land, slab_out, slab, counted, st, base, depth0, wet0, green, plane, pairs, tiles,
     in_sem, gs_sem, gr_sem, hs_sem, hr_sem,
 ):
     gx, gy = lax.axis_index("gx"), lax.axis_index("gy")
@@ -136,7 +136,7 @@
     coarse_rows, coarse_cols = rb_own * ny, cb_own * nx
     ext = rows + 2 * HALO
     ext_tiles = ext // BLOCK
-    my_slot = ((gx // 2) * ny + gy) * 2 + gx % 2
+    my_slot = gy * nx + gx
     fields = (eta, pp, qq)
 
     inputs = [
@@ -164,11 +164,22 @@
 
         lax.fori_loop(1, nx, column, 0)
 
+    def to_band(fn):
+        def one(dx, carry):
+            fn({"gx": wrap(gx + dx, nx), "gy": gy})
+            return carry
+
+        lax.fori_loop(1, nx, one, 0)
+
+    def to_column(fn):
+        for dy in range(1, ny):
+            fn({"gx": gx, "gy": wrap(gy + dy, ny)})
+
     barrier = pltpu.get_barrier_semaphore()
 
-    to_all_others(
-        lambda device: pl.semaphore_signal(barrier, inc=1, device_id=device, device_id_type=MESH)
-    )
+    def greet(device):
+        pl.semaphore_signal(barrier, inc=1, device_id=device, device_id_type=MESH)
+
 
     def target_of(dx, dy):
         return {"gx": wrap(jnp.where(gx + dx < 0, gx + dx + nx, gx + dx), nx), "gy": gy + dy}
@@ -179,6 +190,12 @@
         else:
             beyond = gy + (dy if sending else -dy)
             pl.when((beyond >= 0) & (beyond < ny))(fn)
+
+    to_band(greet)
+    to_column(greet)
+    for dy in (1, -1):
+        when(dy, True, lambda dy=dy: [greet(target_of(dx, dy)) for dx in (1, -1)] and None)
+    greeted = nx + ny - 2 + 2 * jnp.where(gy > 0, 1, 0) + 2 * jnp.where(gy < ny - 1, 1, 0)
 
     planes, layers = (5, 3), (13, 12)
 
@@ -226,14 +243,14 @@
         for j in slots:
             base[j, band(t), :] = pick(source, (lane & -8) + j)
 
-    def send_loads(i, sums):
+    def place_loads(ref, slot, sums):
         spread = None
         for t, total in enumerate(sums):
             total = jnp.broadcast_to(jnp.sum(total, axis=0, keepdims=True), (8, 128)) * (1.0 / (BLOCK * HALF))
             mine = pick(total, (lane & 15) * 8 + sub)
             here = lane // cb_own == t + rb_own * (gx % 2)
             spread = jnp.where(here, mine, 0.0 if spread is None else spread)
-        tiles[i, my_slot] = spread.astype(BF16)
+        ref[slot] = spread.astype(BF16)
 
     def two_parts(x):
         high = x.astype(BF16).astype(F32)
@@ -303,15 +320,23 @@
                 table(j, t, first, depth, wet)
             table(SIDE, t, first, depth, wet)
 
-    def start_interval(i):
-        def send(device):
-            pltpu.make_async_remote_copy(
-                src_ref=tiles.at[i, my_slot], dst_ref=tiles.at[i, my_slot],
-                send_sem=gs_sem.at[i], recv_sem=gr_sem.at[i],
-                device_id=device, device_id_type=MESH,
-            ).start()
-
-        to_all_others(send)
+    def gather(src, dst, group, device):
+        return pltpu.make_async_remote_copy(
+            src_ref=src, dst_ref=dst, send_sem=gs_sem.at[group], recv_sem=gr_sem.at[group],
+            device_id=device, device_id_type=MESH,
+        )
+
+    def band_all():
+        part = plane.at[pl.ds(0, nx - 1)]
+        return gather(part, part, 0, target_of(1, 0))
+
+    def column_all():
+        part = pairs.at[pl.ds(0, ny - 1)]
+        return gather(part, part, 1, target_of(1, 0))
+
+    def everyone():
+        part = tiles.at[pl.ds(0, n - 1)]
+        return gather(part, part, 2, target_of(1, 0))
 
     def start_halos(i):
         for dx in (1, -1):
@@ -328,13 +353,6 @@
         beside_all(i).wait_send()
         for dy in (1, -1):
             when(dy, True, lambda dy=dy: beyond_all(i, dy).wait_send())
-
-    def everyone(i):
-        return pltpu.make_async_remote_copy(
-            src_ref=tiles.at[i, pl.ds(0, n - 1)], dst_ref=tiles.at[i, pl.ds(0, n - 1)],
-            send_sem=gs_sem.at[i], recv_sem=gr_sem.at[i],
-            device_id=target_of(1, 0), device_id_type=MESH,
-        )
 
     def make_turning():
         for e in range(ext_tiles):
@@ -361,8 +379,8 @@
         def green_group(g, carry):
             p = g * 8 + iota((8, pair_rows), 0)
             k = iota((8, pair_rows), 1)
-            s_col = ((p // ny) * 2 + k // per_device) * cb_own + k % cb_own
-            s_row = (p % ny) * rb_own + (k % per_device) // cb_own
+            s_col = ((p % (nx // 2)) * 2 + k // per_device) * cb_own + k % cb_own
+            s_row = (p // (nx // 2)) * rb_own + (k % per_device) // cb_own
             source = unit_vectors(latitude(s_row, coarse_rows), longitude(s_col, coarse_cols))
             source = [jnp.transpose(x) for x in source]
             for j in range(8):
@@ -381,7 +399,9 @@
         group = math.gcd(8, half)
 
         def pair(p):
-            return tiles[i, 2 * p].astype(F32) + tiles[i, 2 * p + 1].astype(F32)
+            if i == 0:
+                return pairs[p // (nx // 2), p % (nx // 2)].astype(F32)
+            return tiles[2 * p].astype(F32) + tiles[2 * p + 1].astype(F32)
 
         def add_group(g, total):
             left, right = [], []
@@ -453,7 +473,7 @@
             value = jnp.where(base[j, band(t), :] > 0.0, value, 0.0)
             total = value if total is None else total + value
         sums.append(total)
-    send_loads(0, sums)
+    place_loads(plane, gx, sums)
     for copy in inputs[3:]:
         copy.wait()
     for f in (1, 2):
@@ -463,21 +483,25 @@
                 fields[f][j, band(t), :] = value * base[j, band(t), :]
     for f in range(4):
         pack(0, f)
-    pl.semaphore_wait(barrier, n - 1)
-    start_interval(0)
+    pl.semaphore_wait(barrier, greeted)
+    to_band(lambda device: gather(plane.at[gx], plane.at[gx], 0, device).start())
     start_halos(0)
 
     make_turning()
     make_green()
+    band_all().wait_recv()
+    for k in range(nx // 2):
+        pairs[gy, k] = (plane[2 * k].astype(F32) + plane[2 * k + 1].astype(F32)).astype(BF16)
+    to_column(lambda device: gather(pairs.at[gy], pairs.at[gy], 1, device).start())
     own_tables(0, depth0, wet0)
     wait_halos(0)
     assemble(0)
     finish_base()
     edge_tables(0, depth0, wet0)
-    everyone(0).wait_recv()
+    column_all().wait_recv()
     load(0)
-    send_loads(1, interval(0))
-    start_interval(1)
+    place_loads(tiles, my_slot, interval(0))
+    to_all_others(lambda device: gather(tiles.at[my_slot], tiles.at[my_slot], 2, device).start())
     for f in range(3):
         pack(1, f)
     start_halos(1)
@@ -486,14 +510,15 @@
     for j in range(8):
         d = base[j, 2 * BLOCK : 2 * BLOCK + rows, :]
         restore[j] = jnp.where(d > 0.0, KEEP ** (2 * STEPS) / jnp.where(d > 0.0, d, 1.0), 0.0)
-    everyone(0).wait_send()
+    band_all().wait_send()
+    column_all().wait_send()
     finish_sends(0)
     wait_halos(1)
     assemble(1)
-    everyone(1).wait_recv()
+    everyone().wait_recv()
     load(1)
     finish_sends(1)
-    everyone(1).wait_send()
+    everyone().wait_send()
 
 
 def finish(
@@ -580,10 +605,12 @@
             pltpu.VMEM(table, F32),
             pltpu.VMEM(table, F32),
             pltpu.VMEM((n // 2, 2 * rb_own * cb_own, 128), BF16),
-            pltpu.VMEM((INTERVALS, n, members, 2 * rb_own * cb_own), BF16),
+            pltpu.VMEM((nx, members, 2 * rb_own * cb_own), BF16),
+            pltpu.VMEM((ny, nx // 2, members, 2 * rb_own * cb_own), BF16),
+            pltpu.VMEM((n, members, 2 * rb_own * cb_own), BF16),
             dma((5,)),
-            dma((INTERVALS,)),
-            dma((INTERVALS,)),
+            dma((3,)),
+            dma((3,)),
             dma((INTERVALS, 3)),
             dma((INTERVALS, 3)),
         ],

time: 22 us -> 21.6 us (0.982)
  Pallas kernels: 21.1 us -> 20.7 us
    pallas_call x1, Pallas kernels: 19.2 us -> 18.8 us  [shards(): pl.pallas_call(functools.partial(kernel, nx, ny, members, rows, cols), ou...]
where the time goes in v2:
time: 21.6 us; the launch traced here: 21.4 us
  Pallas kernels  20.7 us (96%)
  between operations  0.64 us (3%)
    pallas_call x1, Pallas kernels, shards(): pl.pallas_call(functools.partial(kernel, nx, ny, members, rows, cols), ou...  18.8 us
    pallas_call x1, Pallas kernels, shards(): pl.pallas_call(functools.partial(finish, members, rows, cols), out_shape=...  1.94 us

profile of v2, /device:TPU:0, one launch (start us, length us, event | category | flops | bytes accessed | tf_op | source)
XLA Modules:
  0.0 21.4 jit_solution(5823958979372869770)
XLA Ops:
  0.6 18.8 %tide.1 = (f32[9,64,128]{2,1,0:T(8,128)S(1)}, f32[9,64,128]{2,1,0:T(8,128)S(1)}, f32[9,64,128]{2,1,0:T(8,128)S(1)}, f32[4,9,48,128]{3,2,1,0:T(8,128)S(1)}, f32[4...) custom-call(f32[8,32,128]{2,1,0:T(8,128)} %h_in.1, ...), custom_call_target="tpu_custom_call" | custom-call | tf_op jit(solution)/shard_map/tide/pallas_call | solution.py:589
  19.4 1.9 %finish.1 = (f32[8,32,128]{2,1,0:T(8,128)}, f32[8,32,128]{2,1,0:T(8,128)}, f32[8,32,128]{2,1,0:T(8,128)}, f32[8,4,16]{2,1,0:T(4,128)}) custom-call(f32[9,64,128]{2,1,0:T(8,128)S(1)} %get-tuple-element.13.eta_in, f32[9,64,128]{2,1,0:T(8,128)S(1)} %get-tuple-element.14.p_in, f32[9,64,128]{2,1,0:T(8,128)S(1)} %get-tuple-element.15.q_in, ...), custom_call_target="tpu_custom_call" | custom-call | tf_op jit(solution)/shard_map/finish/pallas_call | solution.py:629

commit v3 on v2

--- a/solution.py
+++ b/solution.py
@@ -126,7 +126,7 @@
     h_in, u_in, v_in, d_in, o_in,
     eta, pp, qq, depth1, wet1, turn, restore, fine, l_out,
     in3, in_d, in_o, strips, land, slab_out, slab, counted, st, base, depth0, wet0, green, plane, pairs, tiles,
-    in_sem, gs_sem, gr_sem, hs_sem, hr_sem,
+    in_sem, gs_sem, gr_sem, hs_sem, hr_sem, up_sem,
 ):
     gx, gy = lax.axis_index("gx"), lax.axis_index("gy")
     n = nx * ny
@@ -191,11 +191,33 @@
             beyond = gy + (dy if sending else -dy)
             pl.when((beyond >= 0) & (beyond < ny))(fn)
 
+    def further(up, fn):
+        for dy in range(2, ny):
+            inside = gy + dy < ny if up else gy - dy >= 0
+            pl.when(inside)(lambda dy=dy: fn({"gx": gx, "gy": gy + dy if up else gy - dy}))
+
+    def greet_beyond(dy):
+        for dx in (0, 1, -1):
+            greet(target_of(dx, dy))
+
     to_band(greet)
-    to_column(greet)
     for dy in (1, -1):
-        when(dy, True, lambda dy=dy: [greet(target_of(dx, dy)) for dx in (1, -1)] and None)
-    greeted = nx + ny - 2 + 2 * jnp.where(gy > 0, 1, 0) + 2 * jnp.where(gy < ny - 1, 1, 0)
+        when(dy, True, lambda dy=dy: greet_beyond(dy))
+    further(True, greet)
+
+    def meet():
+        below, above = jnp.where(gy > 0, gy + 2, 0), jnp.where(gy < ny - 1, 3, 0)
+        pl.semaphore_wait(barrier, nx - 1 + below + above)
+        further(
+            False,
+            lambda device: pl.semaphore_signal(up_sem, inc=1, device_id=device, device_id_type=MESH),
+        )
+
+    def hear_answers():
+        pl.when(gy < ny - 2)(lambda: pl.semaphore_wait(up_sem, ny - 2 - gy))
+
+    meets_early = (gx // 2 == nx // 2 - 1) & (gy == ny - 1)
+    pl.when(meets_early)(meet)
 
     planes, layers = (5, 3), (13, 12)
 
@@ -338,9 +360,12 @@
         part = tiles.at[pl.ds(0, n - 1)]
         return gather(part, part, 2, target_of(1, 0))
 
-    def start_halos(i):
+    def start_beside(i):
         for dx in (1, -1):
             beside(i, dx).start()
+
+    def start_halos(i):
+        start_beside(i)
         for dy in (1, -1):
             when(dy, True, lambda dy=dy: start_beyond(i, dy))
 
@@ -474,6 +499,11 @@
             total = value if total is None else total + value
         sums.append(total)
     place_loads(plane, gx, sums)
+
+    def send_band():
+        to_band(lambda device: gather(plane.at[gx], plane.at[gx], 0, device).start())
+
+    pl.when(meets_early)(send_band)
     for copy in inputs[3:]:
         copy.wait()
     for f in (1, 2):
@@ -483,8 +513,12 @@
                 fields[f][j, band(t), :] = value * base[j, band(t), :]
     for f in range(4):
         pack(0, f)
-    pl.semaphore_wait(barrier, greeted)
-    to_band(lambda device: gather(plane.at[gx], plane.at[gx], 0, device).start())
+
+    def meet_late():
+        meet()
+        send_band()
+
+    pl.when(jnp.logical_not(meets_early))(meet_late)
     start_halos(0)
 
     make_turning()
@@ -492,6 +526,7 @@
     band_all().wait_recv()
     for k in range(nx // 2):
         pairs[gy, k] = (plane[2 * k].astype(F32) + plane[2 * k + 1].astype(F32)).astype(BF16)
+    hear_answers()
     to_column(lambda device: gather(pairs.at[gy], pairs.at[gy], 1, device).start())
     own_tables(0, depth0, wet0)
     wait_halos(0)
@@ -515,10 +550,10 @@
     finish_sends(0)
     wait_halos(1)
     assemble(1)
+    finish_sends(1)
+    everyone().wait_send()
     everyone().wait_recv()
     load(1)
-    finish_sends(1)
-    everyone().wait_send()
 
 
 def finish(
@@ -613,6 +648,7 @@
             dma((3,)),
             dma((INTERVALS, 3)),
             dma((INTERVALS, 3)),
+            pltpu.SemaphoreType.REGULAR,
         ],
         compiler_params=pltpu.CompilerParams(
             collective_id=0, has_side_effects=True, vmem_limit_bytes=40 * 1024 * 1024

time: 21.6 us -> 20.8 us (0.963)
  Pallas kernels: 20.7 us -> 19.9 us
    pallas_call x1, Pallas kernels: 18.8 us -> 18 us  [shards(): pl.pallas_call(functools.partial(kernel, nx, ny, members, rows, cols), ou...]
where the time goes in v3:
time: 20.8 us; the launch traced here: 20.6 us
  Pallas kernels  19.9 us (96%)
  between operations  0.64 us (3%)
    pallas_call x1, Pallas kernels, shards(): pl.pallas_call(functools.partial(kernel, nx, ny, members, rows, cols), ou...  18 us
    pallas_call x1, Pallas kernels, shards(): pl.pallas_call(functools.partial(finish, members, rows, cols), out_shape=...  1.94 us

profile of v3, /device:TPU:0, one launch (start us, length us, event | category | flops | bytes accessed | tf_op | source)
XLA Modules:
  0.0 20.6 jit_solution(6255589072403506744)
XLA Ops:
  0.6 18.0 %tide.1 = (f32[9,64,128]{2,1,0:T(8,128)S(1)}, f32[9,64,128]{2,1,0:T(8,128)S(1)}, f32[9,64,128]{2,1,0:T(8,128)S(1)}, f32[4,9,48,128]{3,2,1,0:T(8,128)S(1)}, f32[4...) custom-call(f32[8,32,128]{2,1,0:T(8,128)} %h_in.1, ...), custom_call_target="tpu_custom_call" | custom-call | tf_op jit(solution)/shard_map/tide/pallas_call | solution.py:624
  18.6 1.9 %finish.1 = (f32[8,32,128]{2,1,0:T(8,128)}, f32[8,32,128]{2,1,0:T(8,128)}, f32[8,32,128]{2,1,0:T(8,128)}, f32[8,4,16]{2,1,0:T(4,128)}) custom-call(f32[9,64,128]{2,1,0:T(8,128)S(1)} %get-tuple-element.13.eta_in, f32[9,64,128]{2,1,0:T(8,128)S(1)} %get-tuple-element.14.p_in, f32[9,64,128]{2,1,0:T(8,128)S(1)} %get-tuple-element.15.q_in, ...), custom_call_target="tpu_custom_call" | custom-call | tf_op jit(solution)/shard_map/finish/pallas_call | solution.py:665

commit v4 on v3

--- a/solution.py
+++ b/solution.py
@@ -25,6 +25,7 @@
 BF16 = jnp.bfloat16
 
 SIDE = 8
+TOGETHER = 4
 SLOTS = 9
 
 
@@ -53,20 +54,21 @@
     return jnp.take_along_axis(x, index, axis=1)
 
 
-def exchange(values):
+def exchange(groups):
     lane = lanes()
-    values = list(values)
+    groups = [list(values) for values in groups]
     for bit in range(3):
         step = 1 << bit
         low = (lane & step) == 0
         index = lane ^ step
-        for a in range(8):
-            if a & step:
-                continue
-            b = a | step
-            moved = pick(jnp.where(low, values[b], values[a]), index)
-            values[a], values[b] = jnp.where(low, values[a], moved), jnp.where(low, moved, values[b])
-    return values
+        for values in groups:
+            for a in range(8):
+                if a & step:
+                    continue
+                b = a | step
+                moved = pick(jnp.where(low, values[b], values[a]), index)
+                values[a], values[b] = jnp.where(low, values[a], moved), jnp.where(low, moved, values[b])
+    return groups
 
 
 def band(t):
@@ -80,13 +82,13 @@
 def x_differences(values, with_side=True):
     lane = lanes()
     first, last = lane < 8, lane >= 120
-    edge_east, edge_west = pltpu.roll(values[7], 8, 1), pltpu.roll(values[0], 120, 1)
-    side = values[SIDE]
-    left = [jnp.where(first, pltpu.roll(side, 8, 1), edge_east)] + values[:7]
-    right = values[1:8] + [jnp.where(last, pltpu.roll(side, 120, 1), edge_west)]
+    up_main, up_side = pltpu.roll(values[7], 8, 1), pltpu.roll(values[SIDE], 8, 1)
+    down_main, down_side = pltpu.roll(values[0], 120, 1), pltpu.roll(values[SIDE], 120, 1)
+    left = [jnp.where(first, up_side, up_main)] + values[:7]
+    right = values[1:8] + [jnp.where(last, down_side, down_main)]
     if with_side:
-        left.append(jnp.where(first, edge_east, pltpu.roll(side, 16, 1)))
-        right.append(jnp.where(last, edge_west, pltpu.roll(side, 112, 1)))
+        left.append(jnp.where(first, up_main, up_side))
+        right.append(jnp.where(last, down_main, down_side))
     return [r - l for l, r in zip(left, right)]
 
 
@@ -140,9 +142,10 @@
     fields = (eta, pp, qq)
 
     inputs = [
-        pltpu.make_async_copy(src, dst, in_sem.at[k])
-        for k, (src, dst) in enumerate(
-            ((d_in, in_d), (o_in, in_o), (h_in, in3.at[0]), (u_in, in3.at[1]), (v_in, in3.at[2]))
+        pltpu.make_async_copy(src, dst, done)
+        for src, dst, done in (
+            (d_in, in_d, hs_sem.at[0]), (o_in, in_o, hs_sem.at[1]), (h_in, in3.at[0], hs_sem.at[2]),
+            (u_in, in3.at[1], in_sem.at[0]), (v_in, in3.at[2], in_sem.at[1]),
         )
     ]
     for copy in inputs:
@@ -223,7 +226,7 @@
 
     def remote(src, dst, i, group, dx, dy):
         return pltpu.make_async_remote_copy(
-            src_ref=src, dst_ref=dst, send_sem=hs_sem.at[i, group], recv_sem=hr_sem.at[i, group],
+            src_ref=src, dst_ref=dst, send_sem=hs_sem.at[group], recv_sem=hr_sem.at[i, group],
             device_id=target_of(dx, dy), device_id_type=MESH,
         )
 
@@ -289,11 +292,12 @@
                 both = jnp.concatenate([ref[2 * k, band(t), :], ref[2 * k + 1, band(t), :]], axis=0)
                 slab_out[i, at, 4 * f + k] = both.astype(BF16)
         packed = [None] * rb_own
+        index = (lane & 7) + jnp.where(lane >= 64, cols - 8, 0)
         for j in range(8):
-            index = (lane + (128 - 16 * j - 8)) & 127
+            here = (lane // 8) % 8 == j
             for b in range(rb_own):
                 moved = pick(ref[j, band(b + 1), :], index)
-                packed[b] = moved if j == 0 else jnp.where(lane // 16 == j, moved, packed[b])
+                packed[b] = moved if j == 0 else jnp.where(here, moved, packed[b])
         for b in range(rb_own):
             parts = two_parts(packed[b]) if f == 3 else (packed[b],)
             for k, part in enumerate(parts):
@@ -301,7 +305,7 @@
 
     def side_of(i, t, planes):
         west, east = (sum(land[i, side, t, k].astype(F32) for k in planes) for side in (0, 1))
-        return pick(jnp.where((lane & 8) != 0, east, west), lane ^ 8)
+        return jnp.where(lane >= 64, west, east)
 
     def assemble(i):
         for f, ref in enumerate(fields):
@@ -344,7 +348,7 @@
 
     def gather(src, dst, group, device):
         return pltpu.make_async_remote_copy(
-            src_ref=src, dst_ref=dst, send_sem=gs_sem.at[group], recv_sem=gr_sem.at[group],
+            src_ref=src, dst_ref=dst, send_sem=gs_sem, recv_sem=gr_sem.at[group],
             device_id=device, device_id_type=MESH,
         )
 
@@ -419,7 +423,7 @@
 
         lax.fori_loop(0, n // 16, green_group, 0)
 
-    def load(i):
+    def load(i, ready=None):
         half = n // 4
         group = math.gcd(8, half)
 
@@ -429,14 +433,17 @@
             return tiles[2 * p].astype(F32) + tiles[2 * p + 1].astype(F32)
 
         def add_group(g, total):
-            left, right = [], []
-            for k in range(group):
-                q = g * group + k
-                left.append(jnp.concatenate([pair(q), pair(q + half)], axis=0).astype(BF16))
-                right.append(jnp.concatenate([green[q], green[q + half]], axis=1))
-            return total + jnp.dot(
-                jnp.concatenate(left, axis=1), jnp.concatenate(right, axis=0), preferred_element_type=F32
-            )
+            parts = []
+            for first in range(0, group, max(group // 2, 1)):
+                left, right = [], []
+                for k in range(first, first + max(group // 2, 1)):
+                    q = g * group + k
+                    left.append(jnp.concatenate([pair(q), pair(q + half)], axis=0).astype(BF16))
+                    right.append(jnp.concatenate([green[q], green[q + half]], axis=1))
+                parts.append(
+                    jnp.dot(jnp.concatenate(left, axis=1), jnp.concatenate(right, axis=0), preferred_element_type=F32)
+                )
+            return total + sum(parts)
 
         both = lax.fori_loop(0, half // group, add_group, jnp.zeros((2 * members, 256), F32))
         loading = both[:members, :128] + both[members:, 128:]
@@ -447,10 +454,11 @@
         west = south + cb_own
         east = west + rb_own + 2
         own_member = (lane & 7) == sub
+        sides = []
         for t in range(ext_tiles):
             first = north if t == 0 else south if t == ext_tiles - 1 else (t - 1) * cb_own
             main = pick(loading, lane // 8 + first)
-            side = pick(loading, jnp.where((lane & 8) != 0, west + t, east + t))
+            side = pick(loading, jnp.where(lane >= 64, west + t, east + t))
             both = []
             for value in (main, side):
                 value = jnp.where(own_member, value, 0.0)
@@ -460,9 +468,13 @@
                     value = jnp.where(gy == ny - 1, 0.0, value)
                 both.append(jnp.broadcast_to(jnp.sum(value, axis=0, keepdims=True), (8, 128)))
             fine[t] = both[0]
+            sides.append(both[1])
+        if ready is not None:
+            ready()
+        for t in range(ext_tiles):
             for j in range(8):
-                eta[j, band(t), :] = eta[j, band(t), :] - both[0]
-            eta[SIDE, band(t), :] = eta[SIDE, band(t), :] - both[1]
+                eta[j, band(t), :] = eta[j, band(t), :] - fine[t]
+            eta[SIDE, band(t), :] = eta[SIDE, band(t), :] - sides[t]
 
     def interval(i):
         def step(n, carry):
@@ -492,7 +504,7 @@
         part = slice((t - 1) * BLOCK, t * BLOCK)
         put_base(t, st[part, :] * (HALF * HALF), range(8))
         total = None
-        for j, value in enumerate(exchange([in3[0, m, part, :] for m in range(8)])):
+        for j, value in enumerate(exchange([[in3[0, m, part, :] for m in range(8)]])[0]):
             value = value * HALF
             eta[j, band(t), :] = value
             value = jnp.where(base[j, band(t), :] > 0.0, value, 0.0)
@@ -509,7 +521,7 @@
     for f in (1, 2):
         for t in range(1, ext_tiles - 1):
             part = slice((t - 1) * BLOCK, t * BLOCK)
-            for j, value in enumerate(exchange([in3[f, m, part, :] for m in range(8)])):
+            for j, value in enumerate(exchange([[in3[f, m, part, :] for m in range(8)]])[0]):
                 fields[f][j, band(t), :] = value * base[j, band(t), :]
     for f in range(4):
         pack(0, f)
@@ -527,12 +539,15 @@
     for k in range(nx // 2):
         pairs[gy, k] = (plane[2 * k].astype(F32) + plane[2 * k + 1].astype(F32)).astype(BF16)
     hear_answers()
+    band_all().wait_send()
     to_column(lambda device: gather(pairs.at[gy], pairs.at[gy], 1, device).start())
     own_tables(0, depth0, wet0)
     wait_halos(0)
     assemble(0)
     finish_base()
     edge_tables(0, depth0, wet0)
+    finish_sends(0)
+    column_all().wait_send()
     column_all().wait_recv()
     load(0)
     place_loads(tiles, my_slot, interval(0))
@@ -545,15 +560,15 @@
     for j in range(8):
         d = base[j, 2 * BLOCK : 2 * BLOCK + rows, :]
         restore[j] = jnp.where(d > 0.0, KEEP ** (2 * STEPS) / jnp.where(d > 0.0, d, 1.0), 0.0)
-    band_all().wait_send()
-    column_all().wait_send()
-    finish_sends(0)
-    wait_halos(1)
-    assemble(1)
     finish_sends(1)
     everyone().wait_send()
+
+    def halos_ready():
+        wait_halos(1)
+        assemble(1)
+
     everyone().wait_recv()
-    load(1)
+    load(1, halos_ready)
 
 
 def finish(
@@ -580,23 +595,30 @@
     lax.fori_loop(1, STEPS - 1, step, 0)
     move_flow(ext_tiles, STEPS - 1, True, eta, pp, qq, pp, qq, depth, turn)
     copies = [pltpu.make_async_copy(staged.at[f], out, sem.at[f]) for f, out in ((1, u_out), (2, v_out))]
-    for t in range(rows // BLOCK):
-        part = pl.ds(t * BLOCK, BLOCK)
+    for t in range(rows // (BLOCK * TOGETHER)):
+        part = pl.ds(t * BLOCK * TOGETHER, BLOCK * TOGETHER)
         copies.append(pltpu.make_async_copy(staged.at[0, :, part], h_out.at[:, part], sem.at[4 + t]))
 
-    def place(f, t, values):
-        for m, value in enumerate(exchange(values)):
-            staged[f, m, (t - 1) * BLOCK : t * BLOCK, :] = value
-
-    for f, ref in ((1, pp), (2, qq)):
-        for t in range(1, ext_tiles - 1):
-            part = slice((t - 1) * BLOCK, t * BLOCK)
-            place(f, t, [ref[j, band(t), :] * restore[j, part, :] for j in range(8)])
-        copies[f - 1].start()
-    for t in range(1, ext_tiles - 1):
+    def place(f, first, groups):
+        for k, values in enumerate(exchange(groups)):
+            for m, value in enumerate(values):
+                staged[f, m, (first + k - 1) * BLOCK : (first + k) * BLOCK, :] = value
+
+    def flow(ref, t):
+        return [ref[j, band(t), :] * restore[j, (t - 1) * BLOCK : t * BLOCK, :] for j in range(8)]
+
+    def surface(t):
         change = surface_change(t, STEPS - 1, False, pp, qq, wet)
-        place(0, t, [(eta[j, band(t), :] - change[j] + fine[t]) * (1.0 / HALF) for j in range(8)])
-        copies[1 + t].start()
+        return [(eta[j, band(t), :] - change[j] + fine[t]) * (1.0 / HALF) for j in range(8)]
+
+    own = range(1, ext_tiles - 1, TOGETHER)
+    for f, make in ((1, functools.partial(flow, pp)), (2, functools.partial(flow, qq)), (0, surface)):
+        for first in own:
+            place(f, first, [make(t) for t in range(first, first + TOGETHER)])
+            if f == 0:
+                copies[2 + first // TOGETHER].start()
+        if f > 0:
+            copies[f - 1].start()
     for copy in copies:
         copy.wait()
     l_copy.wait()
@@ -643,10 +665,10 @@
             pltpu.VMEM((nx, members, 2 * rb_own * cb_own), BF16),
             pltpu.VMEM((ny, nx // 2, members, 2 * rb_own * cb_own), BF16),
             pltpu.VMEM((n, members, 2 * rb_own * cb_own), BF16),
-            dma((5,)),
+            dma((2,)),
+            dma,
             dma((3,)),
             dma((3,)),
-            dma((INTERVALS, 3)),
             dma((INTERVALS, 3)),
             pltpu.SemaphoreType.REGULAR,
         ],

time: 20.8 us -> 20.6 us (level)
  no operation moved by 1% of the time
where the time goes in v4:
time: 20.6 us; the launch traced here: 20.4 us
  Pallas kernels  19.8 us (96%)
  between operations  0.64 us (3%)
    pallas_call x1, Pallas kernels, shards(): pl.pallas_call(functools.partial(kernel, nx, ny, members, rows, cols), ou...  17.9 us
    pallas_call x1, Pallas kernels, shards(): pl.pallas_call(functools.partial(finish, members, rows, cols), out_shape=...  1.82 us

profile of v4, /device:TPU:0, one launch (start us, length us, event | category | flops | bytes accessed | tf_op | source)
XLA Modules:
  0.0 20.4 jit_solution(4754141053311879213)
XLA Ops:
  0.6 17.9 %tide.1 = (f32[9,64,128]{2,1,0:T(8,128)S(1)}, f32[9,64,128]{2,1,0:T(8,128)S(1)}, f32[9,64,128]{2,1,0:T(8,128)S(1)}, f32[4,9,48,128]{3,2,1,0:T(8,128)S(1)}, f32[4...) custom-call(f32[8,32,128]{2,1,0:T(8,128)} %h_in.1, ...), custom_call_target="tpu_custom_call" | custom-call | tf_op jit(solution)/shard_map/tide/pallas_call | solution.py:646
  18.6 1.8 %finish.1 = (f32[8,32,128]{2,1,0:T(8,128)}, f32[8,32,128]{2,1,0:T(8,128)}, f32[8,32,128]{2,1,0:T(8,128)}, f32[8,4,16]{2,1,0:T(4,128)}) custom-call(f32[9,64,128]{2,1,0:T(8,128)S(1)} %get-tuple-element.13.eta_in, f32[9,64,128]{2,1,0:T(8,128)S(1)} %get-tuple-element.14.p_in, f32[9,64,128]{2,1,0:T(8,128)S(1)} %get-tuple-element.15.q_in, ...), custom_call_target="tpu_custom_call" | custom-call | tf_op jit(solution)/shard_map/finish/pallas_call | solution.py:687

commit v5 on v4

--- a/solution.py
+++ b/solution.py
@@ -155,17 +155,20 @@
         return jnp.where(index >= size, index - size, index)
 
     def to_all_others(fn):
-        others = [wrap(gy + dy, ny) for dy in range(ny)]
-        for y in others[1:]:
-            fn({"gx": gx, "gy": y})
-
-        def column(dx, carry):
-            x = wrap(gx + dx, nx)
-            for y in others:
-                fn({"gx": x, "gy": y})
+        far = 2 * (nx // 2 - 1 - gx // 2)
+
+        def column(k, carry):
+            x = wrap(far + k, nx)
+
+            def all_rows():
+                for dy in range(ny):
+                    fn({"gx": x, "gy": wrap(ny - 1 - gy + dy, ny)})
+
+            pl.when(x != gx)(all_rows)
             return carry
 
-        lax.fori_loop(1, nx, column, 0)
+        lax.fori_loop(0, nx, column, 0)
+        to_column(fn)
 
     def to_band(fn):
         def one(dx, carry):

time: 20.6 us -> 20.4 us (level)
  no operation moved by 1% of the time
where the time goes in v5:
time: 20.4 us; the launch traced here: 20.2 us
  Pallas kernels  19.6 us (96%)
  between operations  0.64 us (3%)
    pallas_call x1, Pallas kernels, shards(): pl.pallas_call(functools.partial(kernel, nx, ny, members, rows, cols), ou...  17.7 us
    pallas_call x1, Pallas kernels, shards(): pl.pallas_call(functools.partial(finish, members, rows, cols), out_shape=...  1.82 us

profile of v5, /device:TPU:0, one launch (start us, length us, event | category | flops | bytes accessed | tf_op | source)
XLA Modules:
  0.0 20.2 jit_solution(7935126507873905595)
XLA Ops:
  0.6 17.7 %tide.1 = (f32[9,64,128]{2,1,0:T(8,128)S(1)}, f32[9,64,128]{2,1,0:T(8,128)S(1)}, f32[9,64,128]{2,1,0:T(8,128)S(1)}, f32[4,9,48,128]{3,2,1,0:T(8,128)S(1)}, f32[4...) custom-call(f32[8,32,128]{2,1,0:T(8,128)} %h_in.1, ...), custom_call_target="tpu_custom_call" | custom-call | tf_op jit(solution)/shard_map/tide/pallas_call | solution.py:649
  18.4 1.8 %finish.1 = (f32[8,32,128]{2,1,0:T(8,128)}, f32[8,32,128]{2,1,0:T(8,128)}, f32[8,32,128]{2,1,0:T(8,128)}, f32[8,4,16]{2,1,0:T(4,128)}) custom-call(f32[9,64,128]{2,1,0:T(8,128)S(1)} %get-tuple-element.13.eta_in, f32[9,64,128]{2,1,0:T(8,128)S(1)} %get-tuple-element.14.p_in, f32[9,64,128]{2,1,0:T(8,128)S(1)} %get-tuple-element.15.q_in, ...), custom_call_target="tpu_custom_call" | custom-call | tf_op jit(solution)/shard_map/finish/pallas_call | solution.py:690

commit v6 on v5

--- a/solution.py
+++ b/solution.py
@@ -154,9 +154,22 @@
     def wrap(index, size):
         return jnp.where(index >= size, index - size, index)
 
+    far = 2 * (nx // 2 - 1 - gx // 2)
+
+    def to_column(fn):
+        for dy in range(ny):
+            y = wrap(ny - 1 - gy + dy, ny)
+            pl.when(y != gy)(lambda y=y: fn({"gx": gx, "gy": y}))
+
+    def to_band(fn):
+        def one(k, carry):
+            x = wrap(far + k, nx)
+            pl.when(x != gx)(lambda: fn({"gx": x, "gy": gy}))
+            return carry
+
+        lax.fori_loop(0, nx, one, 0)
+
     def to_all_others(fn):
-        far = 2 * (nx // 2 - 1 - gx // 2)
-
         def column(k, carry):
             x = wrap(far + k, nx)
 
@@ -169,17 +182,6 @@
 
         lax.fori_loop(0, nx, column, 0)
         to_column(fn)
-
-    def to_band(fn):
-        def one(dx, carry):
-            fn({"gx": wrap(gx + dx, nx), "gy": gy})
-            return carry
-
-        lax.fori_loop(1, nx, one, 0)
-
-    def to_column(fn):
-        for dy in range(1, ny):
-            fn({"gx": gx, "gy": wrap(gy + dy, ny)})
 
     barrier = pltpu.get_barrier_semaphore()
 
@@ -206,9 +208,9 @@
         for dx in (0, 1, -1):
             greet(target_of(dx, dy))
 
+    for dy in (-1, 1):
+        when(dy, True, lambda dy=dy: greet_beyond(dy))
     to_band(greet)
-    for dy in (1, -1):
-        when(dy, True, lambda dy=dy: greet_beyond(dy))
     further(True, greet)
 
     def meet():

time: 20.4 us -> 20.2 us (level)
  Pallas kernels: 19.6 us -> 19.3 us
    pallas_call x1, Pallas kernels: 17.7 us -> 17.5 us  [shards(): pl.pallas_call(functools.partial(kernel, nx, ny, members, rows, cols), ou...]
where the time goes in v6:
time: 20.2 us; the launch traced here: 20 us
  Pallas kernels  19.3 us (96%)
  between operations  0.64 us (3%)
    pallas_call x1, Pallas kernels, shards(): pl.pallas_call(functools.partial(kernel, nx, ny, members, rows, cols), ou...  17.5 us
    pallas_call x1, Pallas kernels, shards(): pl.pallas_call(functools.partial(finish, members, rows, cols), out_shape=...  1.82 us

profile of v6, /device:TPU:0, one launch (start us, length us, event | category | flops | bytes accessed | tf_op | source)
XLA Modules:
  0.0 20.0 jit_solution(17251297496436395445)
XLA Ops:
  0.6 17.5 %tide.1 = (f32[9,64,128]{2,1,0:T(8,128)S(1)}, f32[9,64,128]{2,1,0:T(8,128)S(1)}, f32[9,64,128]{2,1,0:T(8,128)S(1)}, f32[4,9,48,128]{3,2,1,0:T(8,128)S(1)}, f32[4...) custom-call(f32[8,32,128]{2,1,0:T(8,128)} %h_in.1, ...), custom_call_target="tpu_custom_call" | custom-call | tf_op jit(solution)/shard_map/tide/pallas_call | solution.py:651
  18.2 1.8 %finish.1 = (f32[8,32,128]{2,1,0:T(8,128)}, f32[8,32,128]{2,1,0:T(8,128)}, f32[8,32,128]{2,1,0:T(8,128)}, f32[8,4,16]{2,1,0:T(4,128)}) custom-call(f32[9,64,128]{2,1,0:T(8,128)S(1)} %get-tuple-element.13.eta_in, f32[9,64,128]{2,1,0:T(8,128)S(1)} %get-tuple-element.14.p_in, f32[9,64,128]{2,1,0:T(8,128)S(1)} %get-tuple-element.15.q_in, ...), custom_call_target="tpu_custom_call" | custom-call | tf_op jit(solution)/shard_map/finish/pallas_call | solution.py:692

commit v7 on v6

--- a/solution.py
+++ b/solution.py
@@ -148,9 +148,6 @@
             (u_in, in3.at[1], in_sem.at[0]), (v_in, in3.at[2], in_sem.at[1]),
         )
     ]
-    for copy in inputs:
-        copy.start()
-
     def wrap(index, size):
         return jnp.where(index >= size, index - size, index)
 
@@ -211,6 +208,8 @@
     for dy in (-1, 1):
         when(dy, True, lambda dy=dy: greet_beyond(dy))
     to_band(greet)
+    for copy in inputs:
+        copy.start()
     further(True, greet)
 
     def meet():

time: 20.2 us -> 20.2 us (level)
  no operation moved by 1% of the time
where the time goes in v7:
time: 20.2 us; the launch traced here: 20 us
  Pallas kernels  19.3 us (96%)
  between operations  0.64 us (3%)
    pallas_call x1, Pallas kernels, shards(): pl.pallas_call(functools.partial(kernel, nx, ny, members, rows, cols), ou...  17.5 us
    pallas_call x1, Pallas kernels, shards(): pl.pallas_call(functools.partial(finish, members, rows, cols), out_shape=...  1.82 us

profile of v7, /device:TPU:0, one launch (start us, length us, event | category | flops | bytes accessed | tf_op | source)
XLA Modules:
  0.0 20.0 jit_solution(14541208206400179901)
XLA Ops:
  0.6 17.5 %tide.1 = (f32[9,64,128]{2,1,0:T(8,128)S(1)}, f32[9,64,128]{2,1,0:T(8,128)S(1)}, f32[9,64,128]{2,1,0:T(8,128)S(1)}, f32[4,9,48,128]{3,2,1,0:T(8,128)S(1)}, f32[4...) custom-call(f32[8,32,128]{2,1,0:T(8,128)} %h_in.1, ...), custom_call_target="tpu_custom_call" | custom-call | tf_op jit(solution)/shard_map/tide/pallas_call | solution.py:650
  18.1 1.8 %finish.1 = (f32[8,32,128]{2,1,0:T(8,128)}, f32[8,32,128]{2,1,0:T(8,128)}, f32[8,32,128]{2,1,0:T(8,128)}, f32[8,4,16]{2,1,0:T(4,128)}) custom-call(f32[9,64,128]{2,1,0:T(8,128)S(1)} %get-tuple-element.13.eta_in, f32[9,64,128]{2,1,0:T(8,128)S(1)} %get-tuple-element.14.p_in, f32[9,64,128]{2,1,0:T(8,128)S(1)} %get-tuple-element.15.q_in, ...), custom_call_target="tpu_custom_call" | custom-call | tf_op jit(solution)/shard_map/finish/pallas_call | solution.py:691
